TPU v7x, 32 devices: a whole 2x2x4 slice. The times are simulated.
32 devices in a mesh: leaf: 4 (over x, core), blk: 8 (over z, y).
Axes of the slice: x: 2, y: 2, z: 4, core: 2. Of those that a mesh axis runs over, the one named last changes fastest.
Arguments:
- right_side: float32 [4, 8, 448, 128], P('leaf', 'blk'), may hold values from -6 to 6
- inverse_blocks: bfloat16 [4, 8, 448, 2048], P('leaf', 'blk'), may hold values from -0.125 to 0.125
- coupling: bfloat16 [4, 8, 640, 1024], P('leaf', 'blk'), may hold values from -0.0625 to 0.0625
- update_rows: int32 [10, 1024], replicated, may hold values from 0 to 2047, as said below
Outputs:
- solution: float32 [4, 8, 448, 128], P('leaf', 'blk')
Inputs may be any that keep to these rules, and one draw needn't show every extreme that they name: `update_rows`: the 1024 entries of each row are distinct.
All inputs are finite; a program needn't handle non-finite values.
Results may differ from a plain program's by a relative error of at most 0.0075.
Values may be sent and summed in bfloat16 or wider, within the bound.
No kernel may reach another device: no remote copies, remote signals or barrier semaphores. Data moves between devices by JAX's collectives and lax.ppermute only.
A program may use at most 64 MiB of HBM per device.

v0:
```python
import jax
import jax.numpy as jnp
from jax import lax
from jax.sharding import PartitionSpec as P


def from_partner(shard, axis, distance):
    return lax.ppermute(shard, axis, [(i, i ^ 1 << distance) for i in range(lax.axis_size(axis))])


def group_total(partial_value, level_no, leaf_id, want_full):
    members = partial_value.shape[0]
    member = leaf_id & members - 1
    full_rows = None
    summed = lax.psum_scatter(partial_value, "blk", scatter_dimension=1, tiled=True)
    for bit_no in range(level_no):
        summed = summed + from_partner(summed, "leaf", bit_no)
    own_rows = lax.dynamic_index_in_dim(summed, member, 0, keepdims=False)[0]
    if want_full:
        full_rows = lax.all_gather(summed.astype(jnp.bfloat16), "blk", axis=1, tiled=True)
    if full_rows is not None:
        full_rows = full_rows.reshape(-1, full_rows.shape[-1])
    return (own_rows, full_rows)


def local(right_side, inverse_blocks, coupling, update_rows):
    leaves = lax.axis_size("leaf")
    blocks = lax.axis_size("blk")
    tree_depth = leaves.bit_length() - 1
    leaf_id = lax.axis_index("leaf")
    blk_id = lax.axis_index("blk")
    node_width = inverse_blocks.shape[-1]
    load_cases = right_side.shape[-1]
    local_rhs = right_side[0, 0]
    local_inverse = inverse_blocks[0, 0]
    local_coupling = coupling[0, 0]
    row_counts = [node_width // (blocks << level_no) for level_no in range(tree_depth + 1)]
    row_starts = [sum(row_counts[:level_no]) for level_no in range(tree_depth + 1)]
    coupling_starts = {}
    cursor = 0
    for level_no in range(tree_depth):
        for ancestor in range(level_no + 1, tree_depth + 1):
            coupling_starts[level_no, ancestor] = cursor
            cursor += row_counts[level_no]
    pair_bases = []
    cursor = 0
    for level_no in range(tree_depth + 1):
        pair_bases.append(cursor)
        cursor += (leaves >> level_no) * (tree_depth - level_no)

    def coupling_block(level_no, ancestor):
        coup_start = coupling_starts[level_no, ancestor]
        return local_coupling[coup_start : coup_start + row_counts[level_no]]

    def row_list(level_no, ancestor):
        node_id = leaf_id >> level_no
        pair_row = (
            pair_bases[level_no] + node_id * (tree_depth - level_no) + (ancestor - level_no - 1)
        )
        return lax.dynamic_index_in_dim(update_rows, pair_row, 0, keepdims=False)

    pending = {}
    y_levels = []
    for level_no in range(tree_depth + 1):
        members = 1 << level_no
        row_count = row_counts[level_no]
        row_start = row_starts[level_no]
        member = leaf_id & members - 1
        if level_no == 0:
            residual = lax.all_gather(
                local_rhs[row_start : row_start + row_count].astype(jnp.bfloat16),
                "blk",
                axis=0,
                tiled=True,
            )
        else:
            buffer = pending.get(level_no, jnp.zeros((node_width, load_cases), jnp.float32))
            slot_start = (member * blocks + blk_id) * row_count
            current = lax.dynamic_slice_in_dim(buffer, slot_start, row_count, 0)
            buffer = lax.dynamic_update_slice_in_dim(
                buffer, current + local_rhs[row_start : row_start + row_count], slot_start, 0
            )
            unused_rows, residual = group_total(
                buffer.reshape(members, blocks, row_count, load_cases), level_no, leaf_id, True
            )
        inverse_rows = local_inverse[row_start : row_start + row_count]
        y_rows = jnp.dot(inverse_rows, residual, preferred_element_type=jnp.float32)
        y_levels.append(y_rows)
        y_round = y_rows.astype(jnp.bfloat16)
        for ancestor in range(level_no + 1, tree_depth + 1):
            contrib = lax.dot_general(
                coupling_block(level_no, ancestor),
                y_round,
                (((0,), (0,)), ((), ())),
                preferred_element_type=jnp.float32,
            )
            summed = pending.get(ancestor, jnp.zeros((node_width, load_cases), jnp.float32))
            pending[ancestor] = summed.at[row_list(level_no, ancestor)].add(-contrib)
    solved = {}
    outputs = [None] * (tree_depth + 1)
    for level_no in range(tree_depth, -1, -1):
        members = 1 << level_no
        row_count = row_counts[level_no]
        row_start = row_starts[level_no]
        z_rows = y_levels[level_no]
        for ancestor in range(level_no + 1, tree_depth + 1):
            picked = jnp.take(solved[ancestor], row_list(level_no, ancestor), axis=0)
            z_rows = z_rows - jnp.dot(
                coupling_block(level_no, ancestor), picked, preferred_element_type=jnp.float32
            )
        inverse_rows = local_inverse[row_start : row_start + row_count]
        partial_value = lax.dot_general(
            inverse_rows,
            z_rows.astype(jnp.bfloat16),
            (((0,), (0,)), ((), ())),
            preferred_element_type=jnp.float32,
        )
        own_rows, full_rows = group_total(
            partial_value.reshape(members, blocks, row_count, load_cases),
            level_no,
            leaf_id,
            level_no > 0,
        )
        outputs[level_no] = own_rows
        if level_no > 0:
            solved[level_no] = full_rows
    return jnp.concatenate(outputs, 0)[None, None]


def solution(mesh):
    in_specs = (
        P("leaf", "blk", None, None),
        P("leaf", "blk", None, None),
        P("leaf", "blk", None, None),
        P(),
    )
    out_specs = P("leaf", "blk", None, None)
    return jax.shard_map(local, mesh=mesh, in_specs=in_specs, out_specs=out_specs, check_vma=False)
```

profile of v0, /device:TPU:0, one launch (start us, length us, event | category | flops | bytes accessed | tf_op | source)
XLA Modules:
  0.0 612.2 jit_solution(16145240339841454955)
XLA Ops:
  6.5 1.0 slice.135
  7.6 33.0 %all-gather = bf16[1,1,2048,128]{3,2,1,0:T(8,128)(2,1)S(1)} all-gather(bf16[1,1,256,128]{3,2,1,0:T(8,128)(2,1)S(1)} %slice.135), channel_id=2, replica_groups=mesh['leaf'=4,'blk'=8] {'blk'}, dimensions={2}, use_global_device_ids=true | all-gather | bytes 589824 | tf_op jit(solution)/shard_map/all_gather | solution.py:70
  40.6 1.6 fusion.8
  42.2 0.3 fusion.2
  42.7 1.4 compare_select_fusion.2
  44.2 6.3 %scatter_custom_fusion = f32[2048,128]{1,0:T(8,128)S(1)} fusion(s32[1024]{0:T(1024)S(1)} %bitcast.138, f32[1024,128]{1,0:T(8,128)S(1)} %copy.20, f32[]{:T(128)} %constant.56.clone.1), kind=kCustom, calls=%fused_computation.38 | custom fusion | flops 131072 | bytes 1048580 | tf_op jit(solution)/shard_map/scatter-add | solution.py:98
  50.4 0.9 fusion.57
  51.3 1.0 copy-done.1
  52.4 0.7 dynamic-slice
  53.1 78.9 %all-reduce.7.cloned.1.call-done = f32[2,8,128,128]{3,2,1,0:T(8,128)} async-done(((f32[2,8,128,128]{3,2,1,0:T(8,128)}), f32[2,8,128,128]{3,2,1,0:T(8,128)}) %all-reduce.7.cloned.1.call-update) | async-done | bytes 1048592
  132.0 2.2 constant_dynamic-slice_fusion.5
  134.7 6.5 %scatter_custom_fusion.1 = f32[2048,128]{1,0:T(8,128)S(1)} fusion(s32[1024]{0:T(1024)} %bitcast.137, f32[1024,128]{1,0:T(8,128)S(1)} %copy.21, f32[]{:T(128)} %constant.56.clone.1), kind=kCustom, calls=%fused_computation.36 | custom fusion | flops 131072 | bytes 1049088 | tf_op jit(solution)/shard_map/scatter-add | solution.py:98
  141.3 1.6 add_convert_fusion.1
  142.9 31.4 %all_gather.16 = bf16[2,8,128,128]{3,2,1,0:T(8,128)(2,1)S(1)} all-gather(bf16[2,1,128,128]{3,2,1,0:T(8,128)(2,1)S(1)} %add_convert_fusion.1), channel_id=1, replica_groups=mesh['leaf'=4,'blk'=8] {'blk'}, dimensions={1}, use_global_device_ids=true | all-gather | bytes 589824 | tf_op jit(solution)/shard_map/all_gather | solution.py:20
  174.3 0.3 fusion.16
  174.6 2.0 fusion
  176.6 1.2 copy.22
  177.8 6.4 %scatter_fusion = f32[2048,128]{1,0:T(8,128)S(1)} fusion(f32[2048,128]{1,0:T(8,128)S(1)} %scatter_custom_fusion.1, s32[1024]{0:T(1024)S(1)} %bitcast.136, f32[1024,128]{1,0:T(8,128)S(1)} %copy.22), kind=kCustom, calls=%fused_computation.5 | custom fusion | flops 131072 | bytes 1576960 | tf_op jit(solution)/shard_map/scatter-add | solution.py:98
  184.3 0.8 fusion.58
  185.0 1.0 copy-done
  186.1 77.9 %all-reduce.9.cloned.1.call-done = f32[4,8,64,128]{3,2,1,0:T(8,128)} async-done(((f32[4,8,64,128]{3,2,1,0:T(8,128)}), f32[4,8,64,128]{3,2,1,0:T(8,128)}) %all-reduce.9.cloned.1.call-update) | async-done | bytes 1048592
  264.0 1.6 constant_dynamic-slice_fusion.4
  265.7 1.3 collective-permute-done.1
  267.0 1.6 fusion.75
  268.6 1.5 collective-permute-start.2
  270.1 4.1 collective-permute-done.2
  274.2 31.3 %all_gather.17 = bf16[4,8,64,128]{3,2,1,0:T(8,128)(2,1)S(1)} all-gather(bf16[4,1,64,128]{3,2,1,0:T(8,128)(2,1)S(1)} %add_convert_fusion), channel_id=1, replica_groups=mesh['leaf'=4,'blk'=8] {'blk'}, dimensions={1}, use_global_device_ids=true | all-gather | bytes 589824 | tf_op jit(solution)/shard_map/all_gather | solution.py:20
  305.5 0.5 convolution_bitcast_fusion.1
  306.0 1.4 copy.23
  307.5 78.2 %all-reduce.11.cloned.1.call-done = f32[4,8,64,128]{3,2,1,0:T(8,128)} async-done(((f32[4,8,64,128]{3,2,1,0:T(8,128)}), f32[4,8,64,128]{3,2,1,0:T(8,128)}) %all-reduce.11.cloned.1.call-update) | async-done | bytes 1048592
  385.6 1.6 constant_dynamic-slice_fusion.3
  387.3 1.3 collective-permute-done.3
  388.6 1.6 fusion.74
  390.2 1.5 collective-permute-start.4
  391.8 4.1 collective-permute-done.4
  395.9 31.3 %all_gather.18 = bf16[4,8,64,128]{3,2,1,0:T(8,128)(2,1)S(1)} all-gather(bf16[4,1,64,128]{3,2,1,0:T(8,128)(2,1)S(1)} %get-tuple-element.8), channel_id=1, replica_groups=mesh['leaf'=4,'blk'=8] {'blk'}, dimensions={1}, use_global_device_ids=true | all-gather | bytes 589824 | tf_op jit(solution)/shard_map/all_gather | solution.py:20
  427.1 3.2 gather_fusion
  430.4 2.0 convolution_bitcast_fusion.2
  432.5 1.4 copy.24
  434.0 64.1 %reduce-scatter.12.cloned.1.call-done = f32[2,1,128,128]{3,2,0,1:T(8,128)} async-done(((f32[2,8,128,128]{3,2,0,1:T(8,128)}), f32[2,1,128,128]{3,2,0,1:T(8,128)}) %reduce-scatter.12.cloned.1.call-update) | async-done | bytes 131088 | tf_op jit(solution)/shard_map/reduce_scatter | solution.py:15
  498.1 3.2 gather_fusion.2
  501.4 31.5 %all_gather.19 = bf16[2,8,128,128]{3,2,0,1:T(8,128)(2,1)S(1)} all-gather(bf16[2,1,128,128]{3,2,0,1:T(8,128)(2,1)S(1)} %get-tuple-element.6), channel_id=1, replica_groups=mesh['leaf'=4,'blk'=8] {'blk'}, dimensions={1}, use_global_device_ids=true | all-gather | bytes 589824 | tf_op jit(solution)/shard_map/all_gather | solution.py:20
  532.9 3.2 gather_fusion.1
  536.1 1.5 fusion.4
  537.6 1.8 convolution_bitcast_fusion
  539.4 1.3 copy.31
  540.8 63.3 %reduce-scatter.14.cloned.1.call-done = f32[1,1,256,128]{3,2,1,0:T(8,128)} async-done(((f32[1,8,256,128]{3,2,1,0:T(8,128)}), f32[1,1,256,128]{3,2,1,0:T(8,128)}) %reduce-scatter.14.cloned.1.call-update) | async-done | bytes 131088 | tf_op jit(solution)/shard_map/reduce_scatter | solution.py:15
  604.1 1.6 maximum_bitcast_fusion
  (47 shorter events, 1.4 us)
Async XLA Ops:
  6.5 125.5 %all-reduce.7.cloned.1.call-start = ((), (), s32[]{:S(2)}) async-start(), calls=%async_computation.4 | async-start | bytes 2097152
  6.5 35.7 %copy-start.4 = (bf16[1,1,640,1024]{3,2,1,0:T(8,128)(2,1)S(1)}, bf16[1,1,640,1024]{3,2,1,0:T(8,128)(2,1)}, u32[]{:S(2)}) copy-start(bf16[1,1,640,1024]{3,2,1,0:T(8,128)(2,1)} %param.8) | copy-start | bytes 3932164
  42.2 92.0 %copy-start.5 = (f32[256,128]{1,0:T(8,128)}, f32[256,128]{1,0:T(8,128)S(1)}, u32[]{:S(2)}) copy-start(f32[256,128]{1,0:T(8,128)S(1)} %fusion.8) | copy-start | bytes 393220
  42.7 9.7 %copy-start.8 = (u32[32]{0:T(128)S(1)}, u32[32]{0:T(128)}, u32[]{:S(2)}) copy-start(u32[32]{0:T(128)} %constant.76) | copy-start | bytes 388
  51.3 1.0 copy-start.1
  52.3 211.6 %all-reduce.9.cloned.1.call-start = ((), (), s32[]{:S(2)}) async-start(), calls=%async_computation.5 | async-start | bytes 2097152
  134.2 7.0 %collective-permute-start = (f32[2,1,128,128]{3,2,1,0:T(8,128)}, f32[2,1,128,128]{3,2,1,0:T(8,128)S(1)}, u32[]{:S(2)}, u32[]{:S(2)}) collective-permute-start(f32[2,1,128,128]{3,2,1,0:T(8,128)} %constant_dynamic-slice_fusion.5), channel_id=1, source_target_pairs={{0,8},{8,0},{16,24},{24,16},{1,9},{9,1},{17,25},{25,17},{2,10},{10... | collective-permute-start | bytes 393224 | tf_op jit(solution)/shard_map/ppermute | solution.py:8
  134.5 39.8 %copy-start.2 = (bf16[1,1,448,2048]{3,2,1,0:T(8,128)(2,1)S(1)}, bf16[1,1,448,2048]{3,2,1,0:T(8,128)(2,1)}, u32[]{:S(2)}) copy-start(bf16[1,1,448,2048]{3,2,1,0:T(8,128)(2,1)} %param.7) | copy-start | bytes 5505028
  185.0 1.0 copy-start
  186.1 199.6 %all-reduce.11.cloned.1.call-start = ((), (), s32[]{:S(2)}) async-start(), calls=%async_computation.6 | async-start | bytes 2097152
  265.6 1.4 collective-permute-start.1
  268.6 5.6 collective-permute-start.2
  307.4 190.7 %reduce-scatter.12.cloned.1.call-start = ((), (), s32[]{:S(2)}) async-start(), calls=%async_computation.2 | async-start | bytes 1179648 | tf_op jit(solution)/shard_map/reduce_scatter | solution.py:15
  387.2 1.4 collective-permute-start.3
  390.2 5.6 collective-permute-start.4
  434.0 170.1 %reduce-scatter.14.cloned.1.call-start = ((), (), s32[]{:S(2)}) async-start(), calls=%async_computation.3 | async-start | bytes 1179648 | tf_op jit(solution)/shard_map/reduce_scatter | solution.py:15
  498.1 3.2 copy-start.7
  498.1 3.2 collective-permute-start.5
  532.9 3.2 copy-start.6
  532.9 4.7 copy-start.3
Sparse Core Ops, SparseCore 0:
  52.5 79.4 all-reduce.6
  186.2 77.7 all-reduce.8
  307.5 78.0 all-reduce.10
  434.1 63.9 reduce-scatter.11
  540.9 63.1 reduce-scatter.13
where the time goes:
time: 613 us; the launch traced here: 612 us
  waiting for transfers between devices  373 us (61%)
  blocking collectives  158 us (26%)
  other arithmetic  28.8 us (5%)
  local copies, waits for them, and re-layouts  24.7 us (4%)
  between operations  13.5 us (2%)
  matrix products  10.2 us (2%)
    unnamed x8, waiting for transfers between devices  235 us
    reduce_scatter x2, waiting for transfers between devices, group_total(): lax.psum_scatter(partial_value, 'blk', scatter_dimension=1, tiled=True)  127 us
    all_gather x4, blocking collectives, group_total(): lax.all_gather(summed.astype(jnp.bfloat16), 'blk', axis=1, tiled=True)  125 us
    all_gather x1, blocking collectives, local(): lax.all_gather(local_rhs[row_start:row_start + row_count].astype(jnp.bflo...  33 us
    scatter-add x3, other arithmetic, local(): pending[ancestor] = summed.at[row_list(level_no, ancestor)].add(-contrib)  19.2 us
  transfers between devices with their start and end apart: 11, of which 9 were waited for; matrix products, arithmetic and copies ran while one was open for 2% of the time, Pallas kernels for 0%

commit v1 on v0

--- a/solution.py
+++ b/solution.py
@@ -2,6 +2,12 @@
 import jax.numpy as jnp
 from jax import lax
 from jax.sharding import PartitionSpec as P
+
+
+def gather_by_exchange(x, axis, dim):
+    size = lax.axis_size(axis)
+    repeats = [size if d == dim else 1 for d in range(x.ndim)]
+    return lax.all_to_all(jnp.tile(x, repeats), axis, split_axis=dim, concat_axis=dim, tiled=True)
 
 
 def from_partner(shard, axis, distance):
@@ -17,7 +23,7 @@
         summed = summed + from_partner(summed, "leaf", bit_no)
     own_rows = lax.dynamic_index_in_dim(summed, member, 0, keepdims=False)[0]
     if want_full:
-        full_rows = lax.all_gather(summed.astype(jnp.bfloat16), "blk", axis=1, tiled=True)
+        full_rows = gather_by_exchange(summed.astype(jnp.bfloat16), "blk", 1)
     if full_rows is not None:
         full_rows = full_rows.reshape(-1, full_rows.shape[-1])
     return (own_rows, full_rows)

time: 613 us -> 555 us (0.905)
  blocking collectives: 158 us -> 51 us
  waiting for transfers between devices: 373 us -> 407 us
  starting transfers between devices: 3.38 us -> 15.5 us
    all_gather x4 -> x0, blocking collectives: 125 us -> none  [group_total(): lax.all_gather(summed.astype(jnp.bfloat16), 'blk', axis=1, tiled=True)]
    all_to_all x0 -> x3, waiting for transfers between devices: none -> 32.1 us  [gather_by_exchange(): lax.all_to_all(jnp.tile(x, repeats), axis, split_axis=dim, concat_axis=di...]
    all_to_all x0 -> x1, blocking collectives: none -> 17.9 us  [gather_by_exchange(): lax.all_to_all(jnp.tile(x, repeats), axis, split_axis=dim, concat_axis=di...]
    all_to_all x0 -> x3, starting transfers between devices: none -> 12 us  [gather_by_exchange(): lax.all_to_all(jnp.tile(x, repeats), axis, split_axis=dim, concat_axis=di...]
  transfers between devices with their start and end apart: 11 -> 14, of which waited for: 9 -> 14; matrix products, arithmetic and copies ran while one was open for 2% -> 2% of each run, Pallas kernels for 0% -> 0%
where the time goes in v1:
time: 555 us; the launch traced here: 554 us
  waiting for transfers between devices  407 us (73%)
  blocking collectives  51 us (9%)
  other arithmetic  29.2 us (5%)
  local copies, waits for them, and re-layouts  27.5 us (5%)
  starting transfers between devices  15.5 us (3%)
  between operations  13.5 us (2%)
  matrix products  10.9 us (2%)
    unnamed x8, waiting for transfers between devices  234 us
    reduce_scatter x2, waiting for transfers between devices, group_total(): lax.psum_scatter(partial_value, 'blk', scatter_dimension=1, tiled=True)  127 us
    all_gather x1, blocking collectives, local(): lax.all_gather(local_rhs[row_start:row_start + row_count].astype(jnp.bflo...  33 us
    all_to_all x3, waiting for transfers between devices, gather_by_exchange(): lax.all_to_all(jnp.tile(x, repeats), axis, split_axis=dim, concat_axis=di...  32.1 us
    scatter-add x3, other arithmetic, local(): pending[ancestor] = summed.at[row_list(level_no, ancestor)].add(-contrib)  19.5 us
    all_to_all x1, blocking collectives, gather_by_exchange(): lax.all_to_all(jnp.tile(x, repeats), axis, split_axis=dim, concat_axis=di...  17.9 us
    ppermute x6, waiting for transfers between devices, from_partner(): lax.ppermute(shard, axis, [(i, i ^ 1 << distance) for i in range(lax.axis...  13.7 us
    all_to_all x3, starting transfers between devices, gather_by_exchange(): lax.all_to_all(jnp.tile(x, repeats), axis, split_axis=dim, concat_axis=di...  12 us
  transfers between devices with their start and end apart: 14, of which 14 were waited for; matrix products, arithmetic and copies ran while one was open for 2% of the time, Pallas kernels for 0%

profile of v1, /device:TPU:0, one launch (start us, length us, event | category | flops | bytes accessed | tf_op | source)
XLA Modules:
  0.0 554.1 jit_solution(16046602430832353088)
XLA Ops:
  6.5 1.0 slice.135
  7.6 33.0 %all-gather = bf16[1,1,2048,128]{3,2,1,0:T(8,128)(2,1)S(1)} all-gather(bf16[1,1,256,128]{3,2,1,0:T(8,128)(2,1)S(1)} %slice.135), channel_id=2, replica_groups=mesh['leaf'=4,'blk'=8] {'blk'}, dimensions={2}, use_global_device_ids=true | all-gather | bytes 589824 | tf_op jit(solution)/shard_map/all_gather | solution.py:76
  40.6 1.7 fusion.8
  43.6 6.3 %scatter_custom_fusion = f32[2048,128]{1,0:T(8,128)S(1)} fusion(s32[1024]{0:T(1024)S(1)} %bitcast.151, f32[1024,128]{1,0:T(8,128)S(1)} %copy.31, f32[]{:T(128)} %constant.56.clone.1), kind=kCustom, calls=%fused_computation.38 | custom fusion | flops 131072 | bytes 1048580 | tf_op jit(solution)/shard_map/scatter-add | solution.py:104
  50.8 1.0 copy-done.1
  52.4 79.0 %all-reduce.7.cloned.1.call-done = f32[2,8,128,128]{3,2,1,0:T(8,128)} async-done(((f32[2,8,128,128]{3,2,1,0:T(8,128)}), f32[2,8,128,128]{3,2,1,0:T(8,128)}) %all-reduce.7.cloned.1.call-update) | async-done | bytes 1048592
  131.4 1.5 constant_dynamic-slice_fusion.4
  133.0 1.3 collective-permute-done
  134.4 1.5 fusion.57
  136.8 4.2 all-to-all-start
  141.3 1.0 copy.33
  142.3 6.8 %scatter_custom_fusion.1 = f32[2048,128]{1,0:T(8,128)S(1)} fusion(s32[1024]{0:T(1024)S(1)} %bitcast.150, f32[1024,128]{1,0:T(8,128)} %copy.33, f32[]{:T(128)} %constant.56.clone.1), kind=kCustom, calls=%fused_computation.36 | custom fusion | flops 131072 | bytes 1049088 | tf_op jit(solution)/shard_map/scatter-add | solution.py:104
  149.1 6.7 %all-to-all-done = bf16[2,8,128,128]{3,2,0,1:T(8,128)(2,1)S(1)} async-done(((bf16[2,8,128,128]{3,2,0,1:T(8,128)(2,1)}), bf16[2,8,128,128]{3,2,0,1:T(8,128)(2,1)S(1)}, u32[]{:S(2)}, u32[]{:S(2)}) %all-to-all-start) | async-done | bytes 524320 | tf_op jit(solution)/shard_map/all_to_all | solution.py:10
  156.2 2.0 fusion
  158.2 1.2 copy.34
  159.4 6.4 %scatter_fusion = f32[2048,128]{1,0:T(8,128)S(1)} fusion(f32[2048,128]{1,0:T(8,128)S(1)} %scatter_custom_fusion.1, s32[1024]{0:T(1024)S(1)} %bitcast.149, f32[1024,128]{1,0:T(8,128)S(1)} %copy.34), kind=kCustom, calls=%fused_computation.5 | custom fusion | flops 131072 | bytes 1576960 | tf_op jit(solution)/shard_map/scatter-add | solution.py:104
  166.6 1.0 copy-done
  167.7 77.4 %all-reduce.9.cloned.1.call-done = f32[4,8,64,128]{3,2,1,0:T(8,128)} async-done(((f32[4,8,64,128]{3,2,1,0:T(8,128)}), f32[4,8,64,128]{3,2,1,0:T(8,128)}) %all-reduce.9.cloned.1.call-update) | async-done | bytes 1048592
  245.1 1.5 constant_dynamic-slice_fusion.3
  246.7 1.3 collective-permute-done.1
  248.0 1.5 fusion.75
  249.5 1.5 collective-permute-start.2
  251.1 4.1 collective-permute-done.2
  255.3 17.9 %all_to_all.20 = bf16[4,8,64,128]{3,2,0,1:T(8,128)(2,1)S(1)} all-to-all(bf16[4,8,64,128]{3,2,0,1:T(8,128)(2,1)S(1)} %tile.19), channel_id=1, replica_groups=mesh['leaf'=4,'blk'=8] {'blk'}, dimensions={1} | all-to-all | bytes 1048576 | tf_op jit(solution)/shard_map/all_to_all | solution.py:10
  273.8 1.3 copy.36
  275.2 77.5 %all-reduce.11.cloned.1.call-done = f32[4,8,64,128]{3,2,1,0:T(8,128)} async-done(((f32[4,8,64,128]{3,2,1,0:T(8,128)}), f32[4,8,64,128]{3,2,1,0:T(8,128)}) %all-reduce.11.cloned.1.call-update) | async-done | bytes 1048592
  352.7 1.5 dynamic-slice_bitcast_fusion
  354.3 1.3 collective-permute-done.3
  355.6 1.5 fusion.74
  357.1 1.5 collective-permute-start.4
  358.7 4.1 collective-permute-done.4
  363.7 4.2 all-to-all-start.2
  368.0 13.9 %all-to-all-done.2 = bf16[4,8,64,128]{3,2,0,1:T(8,128)(2,1)S(1)} async-done(((bf16[4,8,64,128]{3,2,0,1:T(8,128)(2,1)}), bf16[4,8,64,128]{3,2,0,1:T(8,128)(2,1)S(1)}, u32[]{:S(2)}, u32[]{:S(2)}) %all-to-all-start.2) | async-done | bytes 524320 | tf_op jit(solution)/shard_map/all_to_all | solution.py:10
  381.9 3.2 gather_fusion
  385.1 2.0 convolution_bitcast_fusion.2
  387.3 1.4 copy.40
  388.8 63.4 %reduce-scatter.12.cloned.1.call-done = f32[2,1,128,128]{3,2,0,1:T(8,128)} async-done(((f32[2,8,128,128]{3,2,0,1:T(8,128)}), f32[2,1,128,128]{3,2,0,1:T(8,128)}) %reduce-scatter.12.cloned.1.call-update) | async-done | bytes 131088 | tf_op jit(solution)/shard_map/reduce_scatter | solution.py:21
  452.1 1.6 collective-permute-done.5
  453.7 0.9 convert_bitcast_fusion
  455.5 3.6 all-to-all-start.3
  459.2 3.2 gather_fusion.2
  462.5 11.5 %all-to-all-done.3 = bf16[2,8,128,128]{3,2,0,1:T(8,128)(2,1)S(1)} async-done(((bf16[2,8,128,128]{3,2,0,1:T(8,128)(2,1)}), bf16[2,8,128,128]{3,2,0,1:T(8,128)(2,1)S(1)}, u32[]{:S(2)}, u32[]{:S(2)}) %all-to-all-start.3) | async-done | bytes 524320 | tf_op jit(solution)/shard_map/all_to_all | solution.py:10
  474.1 3.2 gather_fusion.1
  477.3 2.1 fusion.4
  479.4 1.8 convolution_bitcast_fusion
  481.2 1.3 copy.47
  482.6 63.3 %reduce-scatter.14.cloned.1.call-done = f32[1,1,256,128]{3,2,1,0:T(8,128)} async-done(((f32[1,8,256,128]{3,2,1,0:T(8,128)}), f32[1,1,256,128]{3,2,1,0:T(8,128)}) %reduce-scatter.14.cloned.1.call-update) | async-done | bytes 131088 | tf_op jit(solution)/shard_map/reduce_scatter | solution.py:21
  545.9 1.6 maximum_bitcast_fusion
  (56 shorter events, 8.4 us)
Async XLA Ops:
  6.5 124.9 %all-reduce.7.cloned.1.call-start = ((), (), s32[]{:S(2)}) async-start(), calls=%async_computation.8 | async-start | bytes 2097152
  6.5 35.7 %copy-start.4 = (bf16[1,1,640,1024]{3,2,1,0:T(8,128)(2,1)S(1)}, bf16[1,1,640,1024]{3,2,1,0:T(8,128)(2,1)}, u32[]{:S(2)}) copy-start(bf16[1,1,640,1024]{3,2,1,0:T(8,128)(2,1)} %param.8) | copy-start | bytes 3932164
  42.2 98.8 %copy-start.5 = (f32[256,128]{1,0:T(8,128)}, f32[256,128]{1,0:T(8,128)S(1)}, u32[]{:S(2)}) copy-start(f32[256,128]{1,0:T(8,128)S(1)} %fusion.8) | copy-start | bytes 393220
  42.7 9.1 %copy-start.7 = (u32[32]{0:T(128)S(1)}, u32[32]{0:T(128)}, u32[]{:S(2)}) copy-start(u32[32]{0:T(128)} %constant.76) | copy-start | bytes 388
  50.8 1.0 copy-start.1
  132.9 1.4 collective-permute-start
  136.8 19.0 %all-to-all-start = ((bf16[2,8,128,128]{3,2,0,1:T(8,128)(2,1)}), bf16[2,8,128,128]{3,2,0,1:T(8,128)(2,1)S(1)}, u32[]{:S(2)}, u32[]{:S(2)}) async-start(bf16[2,8,128,128]{3,2,0,1:T(8,128)(2,1)} %tile.17), calls=%async_computation | async-start | bytes 1048576 | tf_op jit(solution)/shard_map/all_to_all | solution.py:10
  141.0 104.1 %all-reduce.9.cloned.1.call-start = ((), (), s32[]{:S(2)}) async-start(), calls=%async_computation.9 | async-start | bytes 2097152
  142.3 13.5 %copy-start.2 = (bf16[1,1,448,2048]{3,2,1,0:T(8,128)(2,1)S(1)}, bf16[1,1,448,2048]{3,2,1,0:T(8,128)(2,1)}, u32[]{:S(2)}) copy-start(bf16[1,1,448,2048]{3,2,1,0:T(8,128)(2,1)} %param.7) | copy-start | bytes 5505028
  166.6 1.0 copy-start
  167.6 185.0 %all-reduce.11.cloned.1.call-start = ((), (), s32[]{:S(2)}) async-start(), calls=%async_computation.10 | async-start | bytes 2097152
  246.6 1.4 collective-permute-start.1
  249.5 5.6 %collective-permute-start.2 = (f32[4,1,64,128]{3,2,1,0:T(8,128)S(1)}, f32[4,1,64,128]{3,2,1,0:T(8,128)S(1)}, u32[]{:S(2)}, u32[]{:S(2)}) collective-permute-start(f32[4,1,64,128]{3,2,1,0:T(8,128)S(1)} %fusion.75), channel_id=1, source_target_pairs={{0,16},{8,24},{16,0},{24,8},{1,17},{9,25},{17,1},{25,9},{2,18},{10... | collective-permute-start | bytes 393224 | tf_op jit(solution)/shard_map/ppermute | solution.py:14
  354.2 1.4 collective-permute-start.3
  357.1 5.6 %collective-permute-start.4 = (f32[4,1,64,128]{3,2,0,1:T(8,128)S(1)}, f32[4,1,64,128]{3,2,0,1:T(8,128)S(1)}, u32[]{:S(2)}, u32[]{:S(2)}) collective-permute-start(f32[4,1,64,128]{3,2,0,1:T(8,128)S(1)} %fusion.74), channel_id=1, source_target_pairs={{0,16},{8,24},{16,0},{24,8},{1,17},{9,25},{17,1},{25,9},{2,18},{10... | collective-permute-start | bytes 393224 | tf_op jit(solution)/shard_map/ppermute | solution.py:14
  363.7 18.2 %all-to-all-start.2 = ((bf16[4,8,64,128]{3,2,0,1:T(8,128)(2,1)}), bf16[4,8,64,128]{3,2,0,1:T(8,128)(2,1)S(1)}, u32[]{:S(2)}, u32[]{:S(2)}) async-start(bf16[4,8,64,128]{3,2,0,1:T(8,128)(2,1)} %tile.41), calls=%async_computation.2 | async-start | bytes 1048576 | tf_op jit(solution)/shard_map/all_to_all | solution.py:10
  367.9 84.2 %reduce-scatter.12.cloned.1.call-start = ((), (), s32[]{:S(2)}) async-start(), calls=%async_computation.6 | async-start | bytes 1179648 | tf_op jit(solution)/shard_map/reduce_scatter | solution.py:21
  452.1 1.6 collective-permute-start.5
  455.5 18.5 %all-to-all-start.3 = ((bf16[2,8,128,128]{3,2,0,1:T(8,128)(2,1)}), bf16[2,8,128,128]{3,2,0,1:T(8,128)(2,1)S(1)}, u32[]{:S(2)}, u32[]{:S(2)}) async-start(bf16[2,8,128,128]{3,2,0,1:T(8,128)(2,1)} %tile.43), calls=%async_computation.4 | async-start | bytes 1048576 | tf_op jit(solution)/shard_map/all_to_all | solution.py:10
  459.1 86.8 %reduce-scatter.14.cloned.1.call-start = ((), (), s32[]{:S(2)}) async-start(), calls=%async_computation.7 | async-start | bytes 1179648 | tf_op jit(solution)/shard_map/reduce_scatter | solution.py:21
  474.1 3.2 copy-start.6
  474.1 5.4 copy-start.3
Sparse Core Ops, SparseCore 0:
  51.9 79.4 all-reduce.6
  167.7 77.2 all-reduce.8
  275.3 77.3 all-reduce.10
  388.9 63.2 reduce-scatter.11
  482.7 63.2 reduce-scatter.13
